TPU v7x, 32 devices: a whole 2x2x4 slice. The times are simulated.
32 devices in a mesh: groups: 2 (over y), rows: 4 (over z), zero: 4 (over x, core).
Axes of the slice: x: 2, y: 2, z: 4, core: 2. Of those that a mesh axis runs over, the one named last changes fastest.
Arguments:
- latents: bfloat16 [8, 320, 32, 128], P(('groups', 'zero'), None, 'rows'), parts along dimension 0, may hold values from -40 to 40
- time_shift: float32 [8, 320], P(('groups', 'zero')), parts along dimension 0, may hold values from -4 to 4
- conv_first: bfloat16 [320, 9, 320], P('zero'), may hold values from -0.109375 to 0.109375
- conv_second: bfloat16 [320, 9, 320], P('zero'), may hold values from -0.1875 to 0.1875
- norm_gains: float32 [2, 320], replicated, may hold values from 0.5 to 1.5
- norm_biases: float32 [2, 320], replicated, may hold values from -3 to 3
- grad_output: bfloat16 [8, 320, 32, 128], P(('groups', 'zero'), None, 'rows'), parts along dimension 0, may hold values from -40 to 40
Outputs:
- block_out: bfloat16 [8, 320, 32, 128], P(('groups', 'zero'), None, 'rows'), parts along dimension 0
- grad_input: bfloat16 [8, 320, 32, 128], P(('groups', 'zero'), None, 'rows'), parts along dimension 0
- grad_time: float32 [8, 320], P(('groups', 'zero')), parts along dimension 0
- grad_conv_first: float32 [640, 9, 320], P(('groups', 'zero')), parts along dimension 0
- grad_conv_second: float32 [640, 9, 320], P(('groups', 'zero')), parts along dimension 0
- grad_norms: float32 [8, 320], P('groups'), parts along dimension 0
There are 2 independent parts, one for each index of `groups`. A program takes and returns all parts, laid end to end along the dimension named above; an argument that names none is the same for every part. Nothing has to cross between parts.
All inputs are finite; a program needn't handle non-finite values.
Results may differ from a plain program's by a relative error of at most 0.0056.
Values may be sent and summed in bfloat16 or wider, within the bound.
A program may use at most 128 MiB of HBM per device.

v0:
```python
import jax
import jax.numpy as jnp
from jax import lax
from jax.sharding import PartitionSpec as P

NORM_GROUPS = 32


EPSILON = 1e-05


def with_halo(value, sides, width):
    for axis, dim in sides:
        devices, length = (lax.axis_size(axis), value.shape[dim])
        up = [(i, (i + 1) % devices) for i in range(devices - 1)]
        down = [(j, i) for i, j in up]
        last = lax.slice_in_dim(value, length - width, length, axis=dim)
        first = lax.slice_in_dim(value, 0, width, axis=dim)
        before = lax.ppermute(last, axis, up)
        after = lax.ppermute(first, axis, down)
        value = jnp.concatenate([before, value, after], axis=dim)
    return value


def shifted_stack(padded, flipped):
    height = padded.shape[2] - 2
    width = padded.shape[3]
    widened = jnp.pad(padded, ((0, 0), (0, 0), (0, 0), (1, 1)))
    slices = [
        widened[:, :, tap_row : tap_row + height, tap_col : tap_col + width]
        for tap_row in range(3)
        for tap_col in range(3)
    ]
    if flipped:
        slices = slices[::-1]
    return jnp.stack(slices, axis=1)


def with_faces(field):
    return with_halo(field, (("rows", 2),), 1)


def group_stats(values):
    images, channels, height, width = values.shape
    grouped = values.reshape(images, NORM_GROUPS, channels // NORM_GROUPS, height, width)
    members = channels // NORM_GROUPS * height * width * lax.axis_size("rows")
    totals, squares = lax.psum(
        (jnp.sum(grouped, axis=(2, 3, 4)), jnp.sum(grouped * grouped, axis=(2, 3, 4))), "rows"
    )
    average = totals / members
    centered = grouped - average[:, :, None, None, None]
    variance = squares / members - average * average
    scaling = lax.rsqrt(variance + EPSILON)
    return ((centered * scaling[:, :, None, None, None]).reshape(values.shape), scaling)


def norm_backward(grad_normed, normed, scaling):
    images, channels, height, width = normed.shape
    shape = (images, NORM_GROUPS, channels // NORM_GROUPS, height, width)
    members = channels // NORM_GROUPS * height * width * lax.axis_size("rows")
    grouped_grad = grad_normed.reshape(shape)
    grouped_norm = normed.reshape(shape)
    group_sum, cross_sum = lax.psum(
        (
            jnp.sum(grouped_grad, axis=(2, 3, 4)),
            jnp.sum(grouped_grad * grouped_norm, axis=(2, 3, 4)),
        ),
        "rows",
    )
    result = scaling[:, :, None, None, None] * (
        grouped_grad
        - (group_sum / members)[:, :, None, None, None]
        - grouped_norm * (cross_sum / members)[:, :, None, None, None]
    )
    return result.reshape(normed.shape)


def silu_slope(pre_values):
    logistic = jax.nn.sigmoid(pre_values)
    return logistic * (1.0 + pre_values * (1.0 - logistic))


def forward_conv(stacked, shard):
    return jnp.einsum(
        "otc,ntchw->nohw",
        lax.all_gather(shard, "zero", axis=0, tiled=True),
        stacked,
        preferred_element_type=jnp.float32,
    )


def backward_conv(stacked_grad, shard):
    return jnp.einsum(
        "otc,ntohw->nchw",
        lax.all_gather(shard, "zero", axis=0, tiled=True),
        stacked_grad,
        preferred_element_type=jnp.float32,
    )


def weight_gradient(cotangent, stacked):
    share = lax.psum_scatter(
        jnp.einsum("nohw,ntchw->otc", cotangent, stacked, preferred_element_type=jnp.float32),
        "zero",
        scatter_dimension=0,
        tiled=True,
    )
    return lax.psum(share, "rows")


def local(latents, time_shift, conv_first, conv_second, norm_gains, norm_biases, grad_output):
    gain_first = norm_gains[0][None, :, None, None]
    gain_second = norm_gains[1][None, :, None, None]
    bias_first = norm_biases[0][None, :, None, None]
    bias_second = norm_biases[1][None, :, None, None]
    normed_first, scale_first = group_stats(latents.astype(jnp.float32))
    pre_first = gain_first * normed_first + bias_first
    act_first = jax.nn.silu(pre_first).astype(jnp.bfloat16)
    stack_first = shifted_stack(with_faces(act_first), False)
    conv_out = forward_conv(stack_first, conv_first)
    hidden = (conv_out + time_shift[:, :, None, None]).astype(jnp.bfloat16)
    normed_second, scale_second = group_stats(hidden.astype(jnp.float32))
    pre_second = gain_second * normed_second + bias_second
    act_second = jax.nn.silu(pre_second).astype(jnp.bfloat16)
    stack_second = shifted_stack(with_faces(act_second), False)
    second_out = forward_conv(stack_second, conv_second)
    block_out = (latents.astype(jnp.float32) + second_out).astype(jnp.bfloat16)
    grad_conv_second = weight_gradient(grad_output, stack_second)
    stack_grad = shifted_stack(with_faces(grad_output), True)
    back_second = backward_conv(stack_grad, conv_second)
    slope_second = back_second * silu_slope(pre_second)
    grad_hidden = norm_backward(gain_second * slope_second, normed_second, scale_second)
    grad_time = lax.psum(jnp.sum(grad_hidden, axis=(2, 3)), "rows")
    hidden_grad = grad_hidden.astype(jnp.bfloat16)
    grad_conv_first = weight_gradient(hidden_grad, stack_first)
    stack_hidden = shifted_stack(with_faces(hidden_grad), True)
    back_first = backward_conv(stack_hidden, conv_first)
    slope_first = back_first * silu_slope(pre_first)
    grad_latent = norm_backward(gain_first * slope_first, normed_first, scale_first)
    grad_input = (grad_output.astype(jnp.float32) + grad_latent).astype(jnp.bfloat16)
    local_terms = jnp.stack(
        [
            jnp.sum(slope_first * normed_first, axis=(0, 2, 3)),
            jnp.sum(slope_first, axis=(0, 2, 3)),
            jnp.sum(slope_second * normed_second, axis=(0, 2, 3)),
            jnp.sum(slope_second, axis=(0, 2, 3)),
        ]
    )
    grad_norms = lax.psum(local_terms, ("rows", "zero"))
    return (block_out, grad_input, grad_time, grad_conv_first, grad_conv_second, grad_norms)


def solution(mesh):
    placed = (
        P(("groups", "zero"), None, "rows", None),
        P(("groups", "zero"), None),
        P("zero", None, None),
        P("zero", None, None),
        P(),
        P(),
        P(("groups", "zero"), None, "rows", None),
    )
    return jax.shard_map(
        local,
        mesh=mesh,
        in_specs=placed,
        out_specs=(
            P(("groups", "zero"), None, "rows", None),
            P(("groups", "zero"), None, "rows", None),
            P(("groups", "zero"), None),
            P(("groups", "zero"), None, None),
            P(("groups", "zero"), None, None),
            P("groups", None),
        ),
        check_vma=False,
    )
```

profile of v0, /device:TPU:0, one launch (start us, length us, event | category | flops | bytes accessed | tf_op | source)
XLA Modules:
  0.0 314.7 jit_solution(3994753162945767644)
XLA Ops:
  8.0 1.4 convert_reduce_fusion
  9.8 13.5 %all-reduce.7 = (f32[1,32]{1,0:T(1,128)S(1)}, f32[1,32]{1,0:T(1,128)S(1)}) all-reduce(f32[1,32]{1,0:T(1,128)S(1)} %bitcast.372, f32[1,32]{1,0:T(1,128)S(1)} %bitcast.371), channel_id=1, replica_groups=mesh['groups'=2,'rows'=4,'zero'=4] {'rows'}, use_global_device_ids=true, to_apply=%region_5.6 | all-reduce | flops 64 | bytes 512 | tf_op jit(solution)/shard_map/psum | solution.py:47
  25.1 1.3 collective-permute-start
  26.4 1.3 collective-permute-start.1
  27.9 4.6 %collective-permute-start.4 = (bf16[1,320,1,128]{3,1,2,0:T(8,128)(2,1)S(1)}, bf16[1,320,1,128]{3,1,2,0:T(8,128)(2,1)S(1)}, u32[]{:S(2)}, u32[]{:S(2)}) collective-permute-start(bf16[1,320,1,128]{3,1,2,0:T(8,128)(2,1)S(1)} %get-tuple-element.56), channel_id=1, source_target_pairs={{0,4},{4,8},{8,12},{1,5},{5,9},{9,13},{2,6},{6,10},{10,14},{3,7},{... | collective-permute-start | bytes 245768 | tf_op jit(solution)/shard_map/ppermute | solution.py:19
  32.4 1.3 collective-permute-start.5
  36.7 2.0 collective-permute-done.5
  48.3 2.6 copy-done.4
  51.8 5.8 %convert_reduce_fusion.1 = (f32[320]{0:T(512)S(1)}, f32[320]{0:T(512)S(1)}, bf16[1,8,128,320]{2,3,1,0:T(8,128)(2,1)S(1)}) fusion(f32[320]{0:T(512)S(1)} %reduce.34, bf16[1,9,320,8,128]{4,2,1,3,0:T(8,128)(2,1)} %copy-done.4, bf16[320,9,320]{2,0,1:T(8,128)(2,1)} %all-gather.3.cloned.1.call-done), kind=kOutput, calls=%fused_computation.26 | convolution fusion | flops 1889402368 | bytes 8400640 | tf_op jit(solution)/shard_map/otc,ntchw->nohw/dot_general | solution.py:84
  58.0 9.6 %all-reduce.6 = (f32[1,32]{1,0:T(1,128)S(1)}, f32[1,32]{1,0:T(1,128)S(1)}) all-reduce(f32[1,32]{1,0:T(1,128)S(1)} %bitcast.373, f32[1,32]{1,0:T(1,128)S(1)} %bitcast.369), channel_id=1, replica_groups=mesh['groups'=2,'rows'=4,'zero'=4] {'rows'}, use_global_device_ids=true, to_apply=%region_11.12 | all-reduce | flops 64 | bytes 512 | tf_op jit(solution)/shard_map/psum | solution.py:47
  68.0 6.4 %fusion.83 = (f32[320]{0:T(512)S(1)}, f32[320]{0:T(512)S(1)}, f32[320]{0:T(512)S(1)}, f32[320]{0:T(512)S(1)}, f32[1,320,8,128]{3,1,2,0:T(8,128)S(1)}) fusion(bf16[1,8,128,320]{2,3,1,0:T(8,128)(2,1)S(1)} %get-tuple-element.66, f32[320]{0:T(512)S(1)} %mul.235, f32[320]{0:T(512)S(1)} %sub.127, f32[320]{0:T(512)S(1)} %get-tuple-element.70, ...), kind=kOutput, calls=%fused_computation.64 | convolution fusion | flops 1893989376 | bytes 9717760 | tf_op jit(solution)/shard_map/otc,ntohw->nchw/dot_general | solution.py:93
  74.8 9.4 %all-reduce.5 = (f32[1,32]{1,0:T(1,128)S(1)}, f32[1,32]{1,0:T(1,128)S(1)}) all-reduce(f32[1,32]{1,0:T(1,128)S(1)} %bitcast.374, f32[1,32]{1,0:T(1,128)S(1)} %bitcast.370), channel_id=1, replica_groups=mesh['groups'=2,'rows'=4,'zero'=4] {'rows'}, use_global_device_ids=true, to_apply=%region_17.18 | all-reduce | flops 64 | bytes 512 | tf_op jit(solution)/shard_map/psum | solution.py:63
  84.6 2.1 fusion.154
  86.7 2.9 collective-permute-start.2
  89.6 1.3 collective-permute-start.3
  91.6 4.3 %collective-permute-done.3 = bf16[1,320,1,128]{3,1,2,0:T(8,128)(2,1)S(1)} collective-permute-done((bf16[1,320,1,128]{3,1,2,0:T(8,128)(2,1)S(1)}, bf16[1,320,1,128]{3,1,2,0:T(8,128)(2,1)S(1)}, u32[]{:S(2)}, u32[]{:S(2)}) %collective-permute-start.3) | collective-permute-done | bytes 81952 | tf_op jit(solution)/shard_map/ppermute | solution.py:20
  98.6 4.8 %fusion.4 = f32[9,320,320,1]{2,1,3,0:T(8,128)} fusion(bf16[1,9,320,8,128]{4,2,3,1,0:T(8,128)(2,1)S(1)} %fusion.131, bf16[320,8,128]{2,1,0:T(8,128)(2,1)S(1)} %bitcast.365), kind=kOutput, calls=%fused_computation.4 | convolution fusion | flops 1887436800 | bytes 10240000 | tf_op jit(solution)/shard_map/nohw,ntchw->otc/dot_general | solution.py:103
  103.5 5.6 %copy.103 = f32[320,2880]{1,0:T(8,128)} copy(f32[320,2880]{0,1:T(8,128)} %bitcast.366) | data formatting | bytes 7372800
  109.1 8.1 %fusion.17 = f32[320,9,320]{2,0,1:T(8,128)} fusion(bf16[1,9,320,8,128]{4,2,1,3,0:T(8,128)(2,1)} %copy-done.4, bf16[1,320,8,128]{3,1,2,0:T(8,128)(2,1)S(1)} %get-tuple-element.52), kind=kOutput, calls=%fused_computation.23 | convolution fusion | flops 1887436800 | bytes 10240000 | tf_op jit(solution)/shard_map/nohw,ntchw->otc/dot_general | solution.py:103
  117.3 1.9 collective-permute-start.6
  119.3 1.5 collective-permute-start.7
  121.3 4.3 %collective-permute-done.7 = bf16[1,320,1,128]{3,1,2,0:T(8,128)(2,1)S(1)} collective-permute-done((bf16[1,320,1,128]{3,1,2,0:T(8,128)(2,1)S(1)}, bf16[1,320,1,128]{3,1,2,0:T(8,128)(2,1)S(1)}, u32[]{:S(2)}, u32[]{:S(2)}) %collective-permute-start.7) | collective-permute-done | bytes 81952 | tf_op jit(solution)/shard_map/ppermute | solution.py:20
  135.4 14.0 %reduce-scatter.7.cloned.1.call-done = f32[80,2880]{1,0:T(8,128)} async-done(((f32[320,2880]{1,0:T(8,128)}), f32[80,2880]{1,0:T(8,128)}) %reduce-scatter.7.cloned.1.call-update) | async-done | bytes 921616
  149.4 2.8 copy.104
  152.1 45.8 %reduce-scatter.5.cloned.1.call-done = f32[80,9,320]{2,0,1:T(8,128)} async-done(((f32[320,9,320]{2,0,1:T(8,128)}), f32[80,9,320]{2,0,1:T(8,128)}) %reduce-scatter.5.cloned.1.call-update) | async-done | bytes 921616 | tf_op jit(solution)/shard_map/reduce_scatter | solution.py:102
  198.0 6.4 %fusion.105 = (f32[320]{0:T(512)S(1)}, f32[320]{0:T(512)S(1)}, f32[320]{0:T(512)S(1)}, f32[320]{0:T(512)S(1)}, f32[1,320,8,128]{3,1,2,0:T(8,128)S(1)}) fusion(f32[320]{0:T(512)S(1)} %mul.226, f32[320]{0:T(512)S(1)} %sub.121, bf16[1,320,8,128]{3,2,1,0:T(8,128)(2,1)S(1)} %copy-done, f32[320]{0:T(512)S(1)} %get-tuple-element.69, ...), kind=kOutput, calls=%fused_computation.86 | convolution fusion | flops 1893989376 | bytes 9717760 | tf_op jit(solution)/shard_map/otc,ntohw->nchw/dot_general | solution.py:93
  204.8 12.6 %all-reduce.4 = (f32[1,32]{1,0:T(1,128)S(1)}, f32[1,32]{1,0:T(1,128)S(1)}, f32[1,320]{1,0:T(1,128)}) all-reduce(f32[1,32]{1,0:T(1,128)S(1)} %bitcast.368, f32[1,32]{1,0:T(1,128)S(1)} %bitcast.367, f32[1,320]{1,0:T(1,128)S(1)} %reduce_sum.224), channel_id=1, replica_groups=mesh['groups'=2,'rows'=4,'zero'=4] {'rows'}, use_global_device_ids=true, to_apply=%region_23.24 | all-reduce | flops 384 | bytes 3072 | tf_op jit(solution)/shard_map/psum | solution.py:63
  218.4 1.3 copy.93
  219.7 5.0 %fusion.59 = bf16[1,320,8,128]{3,1,2,0:T(8,128)(2,1)S(1)} fusion(bf16[1,9,320,8,128]{4,2,3,1,0:T(8,128)(2,1)} %copy-done.5, bf16[320,9,320]{2,0,1:T(8,128)(2,1)S(1)} %copy-done.7, bf16[1,320,8,128]{3,2,1,0:T(8,128)(2,1)S(1)} %copy-done), kind=kOutput, calls=%fused_computation.44 | convolution fusion | flops 1888419840 | bytes 9052160 | tf_op jit(solution)/shard_map/otc,ntchw->nohw/dot_general | solution.py:84
  225.9 33.0 %psum.95 = f32[4,320]{1,0:T(4,128)} all-reduce(f32[4,320]{1,0:T(4,128)S(1)} %pad_maximum_fusion.8), channel_id=1, replica_groups=mesh['groups'=2,'rows'=4,'zero'=4] {'rows','zero'}, use_global_device_ids=true, to_apply=%region_34.35 | all-reduce | flops 1280 | bytes 10240 | tf_op jit(solution)/shard_map/psum | solution.py:149
  259.0 45.2 %all-reduce.11.cloned.1.call-done = (f32[80,9,320]{2,0,1:T(8,128)}, f32[80,9,320]{0,2,1:T(8,128)}) async-done(((f32[80,9,320]{2,0,1:T(8,128)}, f32[80,9,320]{0,2,1:T(8,128)}), (f32[80,9,320]{2,0,1:T(8,128)}, f32[80,9,320]{0,2,1:T(8,128)})) %all-reduce.11.cloned.1.call-update) | async-done | bytes 1843216 | tf_op jit(solution)/shard_map/psum | solution.py:108
  304.2 3.0 copy.94
  (127 shorter events, 35.7 us)
Async XLA Ops:
  7.2 17.3 %copy-start = (bf16[1,320,8,128]{3,2,1,0:T(8,128)(2,1)S(1)}, bf16[1,320,8,128]{3,2,1,0:T(8,128)(2,1)}, u32[]{:S(2)}) copy-start(bf16[1,320,8,128]{3,2,1,0:T(8,128)(2,1)} %param.7) | copy-start | bytes 1966084
  7.2 20.6 %copy-start.1 = (bf16[1,320,8,128]{3,2,1,0:T(8,128)(2,1)S(1)}, bf16[1,320,8,128]{3,2,1,0:T(8,128)(2,1)}, u32[]{:S(2)}) copy-start(bf16[1,320,8,128]{3,2,1,0:T(8,128)(2,1)} %param.13) | copy-start | bytes 1966084
  7.2 44.6 %all-gather.3.cloned.1.call-start = ((), (), s32[]{:S(2)}) async-start(), calls=%async_computation.2 | async-start | bytes 2764800 | tf_op jit(solution)/shard_map/all_gather | solution.py:86
  7.9 60.1 %all-gather.5.cloned.1.call-start = ((), (), s32[]{:S(2)}) async-start(), calls=%async_computation.3 | async-start | bytes 2764800 | tf_op jit(solution)/shard_map/all_gather | solution.py:86
  24.4 9.3 %copy-start.6 = (f32[1,320]{1,0:T(1,128)S(1)}, f32[1,320]{1,0:T(1,128)}, u32[]{:S(2)}) copy-start(f32[1,320]{1,0:T(1,128)} %param.8) | copy-start | bytes 3844
  25.1 8.7 %collective-permute-start = (bf16[1,320,1,128]{3,1,2,0:T(8,128)(2,1)S(1)}, bf16[1,320,1,128]{3,1,2,0:T(8,128)(2,1)S(1)}, u32[]{:S(2)}, u32[]{:S(2)}) collective-permute-start(bf16[1,320,1,128]{3,1,2,0:T(8,128)(2,1)S(1)} %get-tuple-element.60), channel_id=1, source_target_pairs={{0,4},{4,8},{8,12},{1,5},{5,9},{9,13},{2,6},{6,10},{10,14},{3,7},{... | collective-permute-start | bytes 245768 | tf_op jit(solution)/shard_map/ppermute | solution.py:19
  26.4 7.4 %collective-permute-start.1 = (bf16[1,320,1,128]{3,1,2,0:T(8,128)(2,1)S(1)}, bf16[1,320,1,128]{3,1,2,0:T(8,128)(2,1)S(1)}, u32[]{:S(2)}, u32[]{:S(2)}) collective-permute-start(bf16[1,320,1,128]{3,1,2,0:T(8,128)(2,1)S(1)} %get-tuple-element.61), channel_id=1, source_target_pairs={{4,0},{8,4},{12,8},{5,1},{9,5},{13,9},{6,2},{10,6},{14,10},{7,3},{... | collective-permute-start | bytes 245768 | tf_op jit(solution)/shard_map/ppermute | solution.py:20
  27.9 8.9 %collective-permute-start.4 = (bf16[1,320,1,128]{3,1,2,0:T(8,128)(2,1)S(1)}, bf16[1,320,1,128]{3,1,2,0:T(8,128)(2,1)S(1)}, u32[]{:S(2)}, u32[]{:S(2)}) collective-permute-start(bf16[1,320,1,128]{3,1,2,0:T(8,128)(2,1)S(1)} %get-tuple-element.56), channel_id=1, source_target_pairs={{0,4},{4,8},{8,12},{1,5},{5,9},{9,13},{2,6},{6,10},{10,14},{3,7},{... | collective-permute-start | bytes 245768 | tf_op jit(solution)/shard_map/ppermute | solution.py:19
  32.4 6.3 %collective-permute-start.5 = (bf16[1,320,1,128]{3,1,2,0:T(8,128)(2,1)S(1)}, bf16[1,320,1,128]{3,1,2,0:T(8,128)(2,1)S(1)}, u32[]{:S(2)}, u32[]{:S(2)}) collective-permute-start(bf16[1,320,1,128]{3,1,2,0:T(8,128)(2,1)S(1)} %get-tuple-element.57), channel_id=1, source_target_pairs={{4,0},{8,4},{12,8},{5,1},{9,5},{13,9},{6,2},{10,6},{14,10},{7,3},{... | collective-permute-start | bytes 245768 | tf_op jit(solution)/shard_map/ppermute | solution.py:20
  33.7 115.6 %reduce-scatter.7.cloned.1.call-start = ((), (), s32[]{:S(2)}) async-start(), calls=%async_computation.5 | async-start | bytes 4710400
  48.2 2.6 copy-start.4
  57.6 16.8 %copy-start.3 = (bf16[1,8,128,320]{2,3,1,0:T(8,128)(2,1)}, bf16[1,8,128,320]{2,3,1,0:T(8,128)(2,1)S(1)}, u32[]{:S(2)}) copy-start(bf16[1,8,128,320]{2,3,1,0:T(8,128)(2,1)S(1)} %get-tuple-element.66) | copy-start | bytes 1966084
  86.7 5.0 %collective-permute-start.2 = (bf16[1,320,1,128]{3,1,2,0:T(8,128)(2,1)S(1)}, bf16[1,320,1,128]{3,1,2,0:T(8,128)(2,1)S(1)}, u32[]{:S(2)}, u32[]{:S(2)}) collective-permute-start(bf16[1,320,1,128]{3,1,2,0:T(8,128)(2,1)S(1)} %get-tuple-element.58), channel_id=1, source_target_pairs={{0,4},{4,8},{8,12},{1,5},{5,9},{9,13},{2,6},{6,10},{10,14},{3,7},{... | collective-permute-start | bytes 245768 | tf_op jit(solution)/shard_map/ppermute | solution.py:19
  89.6 6.3 %collective-permute-start.3 = (bf16[1,320,1,128]{3,1,2,0:T(8,128)(2,1)S(1)}, bf16[1,320,1,128]{3,1,2,0:T(8,128)(2,1)S(1)}, u32[]{:S(2)}, u32[]{:S(2)}) collective-permute-start(bf16[1,320,1,128]{3,1,2,0:T(8,128)(2,1)S(1)} %get-tuple-element.59), channel_id=1, source_target_pairs={{4,0},{8,4},{12,8},{5,1},{9,5},{13,9},{6,2},{10,6},{14,10},{7,3},{... | collective-permute-start | bytes 245768 | tf_op jit(solution)/shard_map/ppermute | solution.py:20
  98.6 4.9 %copy-start.5 = (bf16[1,9,320,8,128]{4,2,3,1,0:T(8,128)(2,1)}, bf16[1,9,320,8,128]{4,2,3,1,0:T(8,128)(2,1)S(1)}, u32[]{:S(2)}) copy-start(bf16[1,9,320,8,128]{4,2,3,1,0:T(8,128)(2,1)S(1)} %fusion.131) | copy-start | bytes 17694724
  109.1 88.9 %reduce-scatter.5.cloned.1.call-start = ((), (), s32[]{:S(2)}) async-start(), calls=%async_computation.4 | async-start | bytes 5529600 | tf_op jit(solution)/shard_map/reduce_scatter | solution.py:102
  117.3 186.9 %all-reduce.11.cloned.1.call-start = ((), (), s32[]{:S(2)}) async-start(), calls=%async_computation.6 | async-start | bytes 5160960 | tf_op jit(solution)/shard_map/psum | solution.py:108
  117.3 4.0 %collective-permute-start.6 = (bf16[1,320,1,128]{3,1,2,0:T(8,128)(2,1)S(1)}, bf16[1,320,1,128]{3,1,2,0:T(8,128)(2,1)S(1)}, u32[]{:S(2)}, u32[]{:S(2)}) collective-permute-start(bf16[1,320,1,128]{3,1,2,0:T(8,128)(2,1)S(1)} %get-tuple-element.54), channel_id=1, source_target_pairs={{0,4},{4,8},{8,12},{1,5},{5,9},{9,13},{2,6},{6,10},{10,14},{3,7},{... | collective-permute-start | bytes 245768 | tf_op jit(solution)/shard_map/ppermute | solution.py:19
  119.3 6.3 %collective-permute-start.7 = (bf16[1,320,1,128]{3,1,2,0:T(8,128)(2,1)S(1)}, bf16[1,320,1,128]{3,1,2,0:T(8,128)(2,1)S(1)}, u32[]{:S(2)}, u32[]{:S(2)}) collective-permute-start(bf16[1,320,1,128]{3,1,2,0:T(8,128)(2,1)S(1)} %get-tuple-element.55), channel_id=1, source_target_pairs={{4,0},{8,4},{12,8},{5,1},{9,5},{13,9},{6,2},{10,6},{14,10},{7,3},{... | collective-permute-start | bytes 245768 | tf_op jit(solution)/shard_map/ppermute | solution.py:20
  217.8 1.9 copy-start.7
  304.2 3.0 copy-start.2
Sparse Core Ops, SparseCore 0:
  9.6 25.9 all-gather.2
  37.1 23.2 all-gather.4
  109.2 40.1 reduce-scatter.6
  152.0 45.9 reduce-scatter.4
  200.3 103.8 all-reduce.10
where the time goes:
time: 315 us
  waiting for transfers between devices  118 us (37%)
  blocking collectives  78 us (25%)
  local copies, waits for them, and re-layouts  38.1 us (12%)
  matrix products  36.4 us (12%)
  starting transfers between devices  16.3 us (5%)
  between operations  14.3 us (5%)
  other arithmetic  14 us (4%)
    reduce_scatter x1, waiting for transfers between devices, weight_gradient(): lax.psum_scatter(jnp.einsum('nohw,ntchw->otc', cotangent, stacked, prefer...  45.8 us
    psum x1, waiting for transfers between devices, weight_gradient(): return lax.psum(share, 'rows')  45.2 us
    psum x1, blocking collectives, local(): grad_norms = lax.psum(local_terms, ('rows', 'zero'))  33 us
    unnamed x46, local copies, waits for them, and re-layouts  32.3 us
    psum x2, blocking collectives, group_stats(): lax.psum((jnp.sum(grouped, axis=(2, 3, 4)), jnp.sum(grouped * grouped, ax...  23 us
    psum x2, blocking collectives, norm_backward(): lax.psum((jnp.sum(grouped_grad, axis=(2, 3, 4)), jnp.sum(grouped_grad * g...  22 us
    unnamed x6, waiting for transfers between devices  14.7 us
    dot_general x2, matrix products, weight_gradient(): jnp.einsum('nohw,ntchw->otc', cotangent, stacked, preferred_element_type=...  12.9 us
  transfers between devices with their start and end apart: 13, of which 8 were waited for; matrix products, arithmetic and copies ran while one was open for 19% of the time, Pallas kernels for 0%

commit v1 on v0

v1 whole, which is shorter than its diff:
```python
import functools

import jax
import jax.numpy as jnp
from jax import lax
from jax.experimental import pallas as pl
from jax.experimental.pallas import tpu as pltpu
from jax.sharding import PartitionSpec as P

NORM_GROUPS = 32
EPSILON = 1e-05
LANES = 128
F32 = jnp.float32
BF16 = jnp.bfloat16
MESH = pl.DeviceIdType.MESH


def block_kernel(
    x, g, pv, w1s, w2s, pool, spread,
    out, gin, small, dw1, dw2,
    act_stack, mid_stack, cot_stack, wfull1, wfull2, wturn,
    normed1, normed2, back, hgrad, cols, stat, halo_out, halo_in,
    part, core_in, core_keep, x_in, z_out, z_in, z_all, tiny, tiny_x,
    send, recv,
):
    channels, cells = x.shape
    height = cells // LANES
    shard = w1s.shape[0]
    rows = lax.axis_size("rows")
    row = lax.axis_index("rows")
    zero = lax.axis_index("zero")
    core = lax.rem(zero, 2)
    mate = zero + 1 - 2 * core
    over = lax.rem(zero + 2, 4)
    over_mate = lax.rem(mate + 2, 4)
    blocks = channels // shard
    members = float(channels // NORM_GROUPS * cells * rows)
    lane = lax.broadcasted_iota(jnp.int32, (shard, LANES), 1)
    wide = lax.broadcasted_iota(jnp.int32, (channels, LANES), 1)
    counter = [0]

    def number():
        counter[0] += 1
        return counter[0] - 1

    pending = []

    def remote(src, dst, target):
        i = number()
        copy = pltpu.make_async_remote_copy(
            src_ref=src, dst_ref=dst, send_sem=send.at[i], recv_sem=recv.at[i],
            device_id=target, device_id_type=MESH,
        )
        return copy

    def go(src, dst, target):
        copy = remote(src, dst, target)
        copy.start()
        pending.append(copy)
        return copy

    def to_rows(src, dst):
        return [go(src, dst, {"rows": lax.rem(row + d, rows)}) for d in range(1, rows)]

    def chunked(body):
        def step(c, _):
            body(pl.multiple_of(c * shard, shard))
            return 0
        lax.fori_loop(0, blocks, step, 0)

    def put(stack, value, start, p, flip):
        left = jnp.where(lane == 0, 0.0, pltpu.roll(value, 1, 1)).astype(BF16)
        right = jnp.where(lane == LANES - 1, 0.0, pltpu.roll(value, LANES - 1, 1)).astype(BF16)
        slabs = (left, value.astype(BF16), right)
        for ty in range(3):
            h = p - 2 + ty if flip else p - ty
            if 0 <= h < height:
                for tx in range(3):
                    tap = 3 * ty + tx
                    stack[pl.ds(start + tap * channels, shard), h * LANES : (h + 1) * LANES] = (
                        slabs[2 - tx if flip else tx]
                    )

    def line(h):
        return slice(h * LANES, (h + 1) * LANES)

    def halo_start(stage, top, bottom):
        down = remote(bottom, halo_in.at[stage, 0], {"rows": lax.rem(row + 1, rows)})
        up = remote(top, halo_in.at[stage, 1], {"rows": lax.rem(row + rows - 1, rows)})

        @pl.when(row < rows - 1)
        def _():
            down.start()

        @pl.when(row > 0)
        def _():
            up.start()

        return down, up

    def halo_finish(stage, pair, stack, flip):
        down, up = pair

        @pl.when(row > 0)
        def _():
            down.wait_recv()
            up.wait_send()

        @pl.when(row < rows - 1)
        def _():
            up.wait_recv()
            down.wait_send()

        @pl.when(row == 0)
        def _():
            halo_in[stage, 0] = jnp.zeros((channels, LANES), BF16)

        @pl.when(row == rows - 1)
        def _():
            halo_in[stage, 1] = jnp.zeros((channels, LANES), BF16)

        def body(start):
            put(stack, halo_in[stage, 0, pl.ds(start, shard), :].astype(F32), start, 0, flip)
            put(stack, halo_in[stage, 1, pl.ds(start, shard), :].astype(F32), start, height + 1, flip)
        chunked(body)

    def lane_sum(value):
        return jnp.sum(value, axis=1, keepdims=True)

    def stat_start(stage, first, second):
        packed = jnp.where(wide == 0, first, jnp.where(wide == 1, second, 0.0))
        stat[stage, row] = jnp.dot(
            pool[...], packed, precision=lax.Precision.HIGHEST, preferred_element_type=F32
        )
        return to_rows(stat.at[stage, row], stat.at[stage, row])

    def stat_finish(stage, copies):
        for copy in copies:
            copy.wait_recv()
        total = stat[stage, 0]
        for i in range(1, rows):
            total = total + stat[stage, i]
        wide_total = jnp.dot(
            spread[...], total, precision=lax.Precision.HIGHEST, preferred_element_type=F32
        ) / members
        return wide_total[:, 0:1], wide_total[:, 1:2]

    def column(i, value):
        cols[i] = jnp.broadcast_to(value, (channels, LANES))

    def moments(stage, copies, at):
        average, square = stat_finish(stage, copies)
        column(at, average)
        column(at + 1, lax.rsqrt(square - average * average + EPSILON))

    barrier = pltpu.get_barrier_semaphore()
    for d in range(1, rows):
        pl.semaphore_signal(
            barrier, inc=1, device_id={"rows": lax.rem(row + d, rows)}, device_id_type=MESH
        )
    for target in (mate, over):
        pl.semaphore_signal(barrier, inc=1, device_id={"zero": target}, device_id_type=MESH)

    SUM_A, SUM_B, SUM_C, SUM_D, SUM_T = 13, 14, 15, 16, 17
    for i in range(5):
        column(8 + i, pv[:, i : i + 1])

    def first_sums(start):
        total = jnp.zeros((shard, LANES), F32)
        square = total
        for h in range(height):
            value = x[pl.ds(start, shard), line(h)].astype(F32)
            total = total + value
            square = square + value * value
        cols[SUM_A, pl.ds(start, shard), :] = total
        cols[SUM_B, pl.ds(start, shard), :] = square
    chunked(first_sums)
    s0, s1 = lane_sum(cols[SUM_A]), lane_sum(cols[SUM_B])

    pl.semaphore_wait(barrier, rows - 1 + 2)
    stat0 = stat_start(0, s0, s1)
    halo_g = halo_start(0, g.at[:, 0:LANES], g.at[:, (height - 1) * LANES : height * LANES])

    def gather_start(own, full):
        near = go(own, full.at[zero], {"zero": mate})
        far = go(own, full.at[zero], {"zero": over})
        return near, far

    def gather_pass(full, far):
        far.wait_recv()
        return go(full.at[over], full.at[over], {"zero": mate})

    gather1 = gather_start(w1s, wfull1)
    gather2 = gather_start(w2s, wfull2)
    wfull1[zero] = w1s[...]
    wfull2[zero] = w2s[...]

    moments(0, stat0, 0)

    def first_act(start):
        at = pl.ds(start, shard)
        for h in range(height):
            normed = (x[at, line(h)].astype(F32) - cols[0, at, :]) * cols[1, at, :]
            normed1[at, line(h)] = normed
            pre = cols[8, at, :] * normed + cols[9, at, :]
            act = (pre / (1.0 + jnp.exp(-pre))).astype(BF16).astype(F32)
            put(act_stack, act, start, h + 1, False)
            if h == 0:
                halo_out[0, 0, at, :] = act.astype(BF16)
            if h == height - 1:
                halo_out[0, 1, at, :] = act.astype(BF16)
    chunked(first_act)
    halo_a = halo_start(1, halo_out.at[0, 0], halo_out.at[0, 1])

    def cot_fill(start):
        for h in range(height):
            put(cot_stack, g[pl.ds(start, shard), line(h)].astype(F32), start, h + 1, True)
    chunked(cot_fill)
    halo_finish(0, halo_g, cot_stack, True)
    pass1 = gather_pass(wfull1, gather1[1])
    halo_finish(1, halo_a, act_stack, False)
    gather1[0].wait_recv()
    pass1.wait_recv()

    TILE = 256

    def tiles(body):
        def step(i, _):
            body(pl.ds(pl.multiple_of(i * TILE, TILE), TILE))
            return 0
        lax.fori_loop(0, cells // TILE, step, 0)

    def conv(full, stack, emit):
        def tile(at):
            weights = full[...].reshape(channels, full.shape[2])
            emit(at, jnp.dot(weights, stack[:, at], preferred_element_type=F32))
        tiles(tile)

    def emit_hidden(at, value):
        shift = cols[12][:, 0:1]
        normed2[:, at] = (value + shift).astype(BF16).astype(F32)
    conv(wfull1, act_stack, emit_hidden)

    def second_sums(start):
        total = jnp.zeros((shard, LANES), F32)
        square = total
        for h in range(height):
            value = normed2[pl.ds(start, shard), line(h)]
            total = total + value
            square = square + value * value
        cols[SUM_A, pl.ds(start, shard), :] = total
        cols[SUM_B, pl.ds(start, shard), :] = square
    chunked(second_sums)
    stat1 = stat_start(1, lane_sum(cols[SUM_A]), lane_sum(cols[SUM_B]))

    PAIR = 2 * channels

    def turn(full):
        depth = full.shape[2]
        for begin in range(0, depth, PAIR):
            end = min(begin + PAIR, depth)
            weights = full[:, :, begin:end].reshape(channels, end - begin)
            wturn[begin:end, :] = weights.T

    def conv_back(stack):
        def tile(at):
            total = jnp.zeros((channels, TILE), F32)
            for tap in range(9):
                span = slice(tap * channels, (tap + 1) * channels)
                total = total + jnp.dot(wturn[span, :], stack[span, at], preferred_element_type=F32)
            back[:, at] = total
        tiles(tile)

    pass2 = gather_pass(wfull2, gather2[1])
    gather2[0].wait_recv()
    pass2.wait_recv()
    turn(wfull2)
    conv_back(cot_stack)
    moments(1, stat1, 2)

    def second_act(start):
        at = pl.ds(start, shard)
        sums = [jnp.zeros((shard, LANES), F32)] * 2
        for h in range(height):
            normed = (normed2[at, line(h)] - cols[2, at, :]) * cols[3, at, :]
            normed2[at, line(h)] = normed
            pre = cols[10, at, :] * normed + cols[11, at, :]
            q = 1.0 / (1.0 + jnp.exp(-pre))
            act = (pre * q).astype(BF16).astype(F32)
            slope = back[at, line(h)] * (q * (1.0 + pre * (1.0 - q)))
            back[at, line(h)] = slope
            sums = [sums[0] + slope * normed, sums[1] + slope]
            put(mid_stack, act, start, h + 1, False)
            if h == 0:
                halo_out[1, 0, at, :] = act.astype(BF16)
            if h == height - 1:
                halo_out[1, 1, at, :] = act.astype(BF16)
        cols[SUM_C, at, :] = sums[0]
        cols[SUM_D, at, :] = sums[1]
    chunked(second_act)
    halo_b = halo_start(2, halo_out.at[1, 0], halo_out.at[1, 1])
    gain_cross2, bias_sum2 = lane_sum(cols[SUM_C]), lane_sum(cols[SUM_D])
    stat2 = stat_start(2, pv[:, 2:3] * bias_sum2, pv[:, 2:3] * gain_cross2)
    halo_finish(2, halo_b, mid_stack, False)

    depth = w1s.shape[1]

    def weight_grad(which, cot, stack):
        for begin in range(0, depth, PAIR):
            end = min(begin + PAIR, depth)
            value = lax.dot_general(
                cot[...], stack[begin:end, :], (((1,), (1,)), ((), ())), preferred_element_type=F32
            )
            part[which, :, :, begin:end] = value.astype(BF16).reshape(blocks, shard, end - begin)
        return [
            go(part.at[which, mate], core_in.at[which, 0], {"zero": mate}),
            go(part.at[which, over_mate], core_in.at[which, 1], {"zero": mate}),
        ]

    def reduce_core(which, copies):
        for copy in copies:
            copy.wait_recv()
        core_keep[which] = (
            part[which, over].astype(F32) + core_in[which, 1].astype(F32)
        ).astype(BF16)
        return go(core_keep.at[which], x_in.at[which], {"zero": over})

    piece = z_out.shape[3]

    def reduce_over(which, copy):
        copy.wait_recv()
        value = (
            part[which, zero].astype(F32)
            + core_in[which, 0].astype(F32)
            + x_in[which].astype(F32)
        ).astype(BF16)
        for q in range(-(-depth // piece)):
            end = min((q + 1) * piece, depth)
            z_out[which, q, :, : end - q * piece] = value[:, q * piece : end]
        copies = []
        for d in range(1, rows):
            to = lax.rem(row + d, rows)
            copies.append(go(z_out.at[which, to], z_in.at[which, row], {"rows": to}))
        return copies

    def reduce_rows(which, copies):
        for copy in copies:
            copy.wait_recv()
        z_in[which, row] = z_out[which, row]
        total = z_in[which, 0].astype(F32)
        for i in range(1, rows):
            total = total + z_in[which, i].astype(F32)
        z_all[which, row] = total.astype(BF16)
        return to_rows(z_all.at[which, row], z_all.at[which, row])

    def reduce_finish(which, copies, target):
        for copy in copies:
            copy.wait_recv()
        for q in range(-(-depth // piece)):
            end = min((q + 1) * piece, depth)
            target[:, q * piece : end] = z_all[which, q, :, : end - q * piece].astype(F32)

    grad2 = weight_grad(1, g, mid_stack)

    average, cross = stat_finish(2, stat2)
    column(4, average)
    column(5, cross)

    def hidden_back(start):
        at = pl.ds(start, shard)
        total = jnp.zeros((shard, LANES), F32)
        for h in range(height):
            value = cols[3, at, :] * (
                cols[10, at, :] * back[at, line(h)]
                - cols[4, at, :]
                - normed2[at, line(h)] * cols[5, at, :]
            )
            total = total + value
            rounded = value.astype(BF16)
            hgrad[at, line(h)] = rounded
            put(cot_stack, rounded.astype(F32), start, h + 1, True)
            if h == 0:
                halo_out[2, 0, at, :] = rounded
            if h == height - 1:
                halo_out[2, 1, at, :] = rounded
        cols[SUM_T, at, :] = total
    chunked(hidden_back)
    halo_h = halo_start(3, halo_out.at[2, 0], halo_out.at[2, 1])
    time_sum = lane_sum(cols[SUM_T])

    grad2 = reduce_core(1, grad2)
    grad1 = weight_grad(0, hgrad, act_stack)
    turn(wfull1)
    halo_finish(3, halo_h, cot_stack, True)
    conv_back(cot_stack)
    grad1 = reduce_core(0, grad1)
    grad2 = reduce_over(1, grad2)

    def first_slope(start):
        at = pl.ds(start, shard)
        sums = [jnp.zeros((shard, LANES), F32)] * 2
        for h in range(height):
            normed = normed1[at, line(h)]
            pre = cols[8, at, :] * normed + cols[9, at, :]
            q = 1.0 / (1.0 + jnp.exp(-pre))
            slope = back[at, line(h)] * (q * (1.0 + pre * (1.0 - q)))
            back[at, line(h)] = slope
            sums = [sums[0] + slope * normed, sums[1] + slope]
        cols[SUM_A, at, :] = sums[0]
        cols[SUM_B, at, :] = sums[1]
    chunked(first_slope)
    gain_cross1, bias_sum1 = lane_sum(cols[SUM_A]), lane_sum(cols[SUM_B])
    stat3 = stat_start(3, pv[:, 0:1] * bias_sum1, pv[:, 0:1] * gain_cross1)
    packed = jnp.zeros((channels, LANES), F32)
    for i, value in enumerate((time_sum, gain_cross1, bias_sum1, gain_cross2, bias_sum2)):
        packed = jnp.where(wide == i, value, packed)
    fill = jnp.zeros((tiny.shape[2] - channels, LANES), F32)
    tiny[row] = jnp.concatenate([packed, fill], axis=0).T[:8, :]
    tiny_rows = to_rows(tiny.at[row], tiny.at[row])

    def emit_out(at, value):
        out[:, at] = (x[:, at].astype(F32) + value).astype(BF16)
    conv(wfull2, mid_stack, emit_out)

    grad1 = reduce_over(0, grad1)
    average, cross = stat_finish(3, stat3)
    column(6, average)
    column(7, cross)

    for copy in tiny_rows:
        copy.wait_recv()
    total = tiny[0]
    for i in range(1, rows):
        total = total + tiny[i]
    tiny_x[0] = total
    first_hop = go(tiny_x.at[0], tiny_x.at[1], {"zero": mate})
    grad2 = reduce_rows(1, grad2)

    def input_back(start):
        at = pl.ds(start, shard)
        for h in range(height):
            value = cols[1, at, :] * (
                cols[8, at, :] * back[at, line(h)]
                - cols[6, at, :]
                - normed1[at, line(h)] * cols[7, at, :]
            )
            gin[at, line(h)] = (g[at, line(h)].astype(F32) + value).astype(BF16)
    chunked(input_back)

    first_hop.wait_recv()
    tiny_x[2] = total + tiny_x[1]
    second_hop = go(tiny_x.at[2], tiny_x.at[3], {"zero": over})
    grad1 = reduce_rows(0, grad1)
    second_hop.wait_recv()
    pick = lax.broadcasted_iota(jnp.int32, total.shape, 0)
    small[...] = jnp.where(pick == 0, total, tiny_x[2] + tiny_x[3])
    reduce_finish(1, grad2, dw2)
    reduce_finish(0, grad1, dw1)
    for copy in pending:
        copy.wait_send()


def local(latents, time_shift, conv_first, conv_second, norm_gains, norm_biases, grad_output):
    _, channels, height, width = latents.shape
    cells = height * width
    shard, taps, _ = conv_first.shape
    depth = taps * channels
    rows = lax.axis_size("rows")
    blocks = channels // shard
    vectors = jnp.stack(
        [norm_gains[0], norm_biases[0], norm_gains[1], norm_biases[1], time_shift[0]]
        + [jnp.zeros((channels,), F32)] * 3,
        axis=1,
    )
    group = jnp.arange(channels) // (channels // NORM_GROUPS)
    pool = (group[None, :] == jnp.arange(NORM_GROUPS)[:, None]).astype(F32)
    piece = -(-depth // (rows * LANES)) * LANES
    padded = -(-channels // LANES) * LANES
    vmem = pl.BlockSpec(memory_space=pltpu.VMEM)
    copies = 4 * (rows - 1) + 8 + 6 + 6 + 5 * (rows - 1) + 8
    field = jax.ShapeDtypeStruct((channels, cells), BF16)
    grads = jax.ShapeDtypeStruct((shard, depth), F32)
    out, gin, small, dw1, dw2 = pl.pallas_call(
        block_kernel,
        out_shape=(field, field, jax.ShapeDtypeStruct((8, padded), F32), grads, grads),
        in_specs=[vmem] * 7,
        out_specs=(vmem,) * 5,
        scratch_shapes=[
            pltpu.VMEM((depth, cells), BF16),
            pltpu.VMEM((depth, cells), BF16),
            pltpu.VMEM((depth, cells), BF16),
            pltpu.VMEM((blocks, shard, depth), BF16),
            pltpu.VMEM((blocks, shard, depth), BF16),
            pltpu.VMEM((depth, channels), BF16),
            pltpu.VMEM((channels, cells), F32),
            pltpu.VMEM((channels, cells), F32),
            pltpu.VMEM((channels, cells), F32),
            pltpu.VMEM((channels, cells), BF16),
            pltpu.VMEM((18, channels, LANES), F32),
            pltpu.VMEM((4, rows, NORM_GROUPS, LANES), F32),
            pltpu.VMEM((3, 2, channels, LANES), BF16),
            pltpu.VMEM((4, 2, channels, LANES), BF16),
            pltpu.VMEM((2, blocks, shard, depth), BF16),
            pltpu.VMEM((2, 2, shard, depth), BF16),
            pltpu.VMEM((2, shard, depth), BF16),
            pltpu.VMEM((2, shard, depth), BF16),
            pltpu.VMEM((2, rows, shard, piece), BF16),
            pltpu.VMEM((2, rows, shard, piece), BF16),
            pltpu.VMEM((2, rows, shard, piece), BF16),
            pltpu.VMEM((rows, 8, padded), F32),
            pltpu.VMEM((4, 8, padded), F32),
            pltpu.SemaphoreType.DMA((copies,)),
            pltpu.SemaphoreType.DMA((copies,)),
        ],
        compiler_params=pltpu.CompilerParams(
            collective_id=0, has_side_effects=True, vmem_limit_bytes=60 * 1024 * 1024
        ),
    )(
        latents.reshape(channels, cells),
        grad_output.reshape(channels, cells),
        vectors,
        conv_first.reshape(shard, depth),
        conv_second.reshape(shard, depth),
        pool,
        pool.T,
    )
    return (
        out.reshape(latents.shape),
        gin.reshape(latents.shape),
        small[0:1, :channels],
        dw1.reshape(conv_first.shape),
        dw2.reshape(conv_second.shape),
        small[1:5, :channels],
    )


def solution(mesh):
    placed = (
        P(("groups", "zero"), None, "rows", None),
        P(("groups", "zero"), None),
        P("zero", None, None),
        P("zero", None, None),
        P(),
        P(),
        P(("groups", "zero"), None, "rows", None),
    )
    return jax.shard_map(
        local,
        mesh=mesh,
        in_specs=placed,
        out_specs=(
            P(("groups", "zero"), None, "rows", None),
            P(("groups", "zero"), None, "rows", None),
            P(("groups", "zero"), None),
            P(("groups", "zero"), None, None),
            P(("groups", "zero"), None, None),
            P("groups", None),
        ),
        check_vma=False,
    )
```

time: 315 us -> 124 us (0.39)
  waiting for transfers between devices: 118 us -> 0 us
  Pallas kernels: 0 us -> 105 us
  blocking collectives: 78 us -> 0 us
  matrix products: 36.4 us -> 0 us
  local copies, waits for them, and re-layouts: 38.1 us -> 16.9 us
  starting transfers between devices: 16.3 us -> 0 us
  between operations: 14.3 us -> 0.72 us
  other arithmetic: 14 us -> 1.41 us
    pallas_call x0 -> x1, Pallas kernels: none -> 105 us  [local(): pl.pallas_call(block_kernel, out_shape=(field, field, jax.ShapeDtypeStruc...]
    psum x5 -> x0, blocking collectives: 78 us -> none  [the longest x1 33 us: local(): grad_norms = lax.psum(local_terms, ('rows', 'zero'))]
    reduce_scatter x1 -> x0, waiting for transfers between devices: 45.8 us -> none  [weight_gradient(): lax.psum_scatter(jnp.einsum('nohw,ntchw->otc', cotangent, stacked, prefer...]
    psum x1 -> x0, waiting for transfers between devices: 45.2 us -> none  [weight_gradient(): return lax.psum(share, 'rows')]
    dot_general x6 -> x0, matrix products: 36.4 us -> none  [the longest x2 12.9 us: weight_gradient(): jnp.einsum('nohw,ntchw->otc', cotangent, stacked, preferred_element_type=...]
    unnamed x46 -> x18, local copies, waits for them, and re-layouts: 32.3 us -> 9.08 us
    ppermute x8 -> x0, starting transfers between devices: 16.1 us -> none  [the longest x4 10.7 us: with_halo(): before = lax.ppermute(last, axis, up)]
    unnamed x6 -> x0, waiting for transfers between devices: 14.7 us -> none
  transfers between devices with their start and end apart: 13 -> 0, of which waited for: 8 -> 0; matrix products, arithmetic and copies ran while one was open for 19% -> 0% of each run, Pallas kernels for 0% -> 0%
where the time goes in v1:
time: 124 us
  Pallas kernels  105 us (85%)
  local copies, waits for them, and re-layouts  16.9 us (14%)
  other arithmetic  1.41 us (1%)
    pallas_call x1, Pallas kernels, local(): pl.pallas_call(block_kernel, out_shape=(field, field, jax.ShapeDtypeStruc...  105 us
    unnamed x18, local copies, waits for them, and re-layouts  9.08 us

profile of v1, /device:TPU:0, one launch (start us, length us, event | category | flops | bytes accessed | tf_op | source)
XLA Modules:
  0.0 123.7 jit_solution(8720167190636107391)
XLA Ops:
  0.6 0.0 copy-start.4
  0.7 0.8 slice_bitcast_fusion
  1.5 0.7 stack.7
  2.2 0.6 fusion.1.pool
  2.8 0.8 copy.32.pv
  3.6 0.8 fusion.spread
  4.4 1.4 %copy.30 = bf16[80,9,320]{0,2,1:T(8,128)(2,1)S(1)} copy(bf16[80,9,320]{2,0,1:T(8,128)(2,1)} %param.9) | data formatting | bytes 921600 | tf_op args[2]
  5.8 1.0 copy.33.w1s
  6.9 0.0 copy-done.4
  6.9 0.0 copy-start.2
  6.9 0.0 copy-start.3
  6.9 0.4 copy.31
  7.3 1.1 copy.34.w2s
  8.3 0.0 copy-done.2
  8.3 0.0 copy-done.3
  8.3 1.4 %copy_bitcast_fusion = (bf16[320,1024]{1,0:T(8,128)(2,1)}, bf16[320,1024]{1,0:T(8,128)(2,1)}) fusion(bf16[40,8,8,128]{3,2,1,0:T(8,128)(2,1)S(1)} %bitcast.31, bf16[40,8,8,128]{3,2,1,0:T(8,128)(2,1)S(1)} %bitcast.32), kind=kLoop, calls=%fused_computation | loop fusion | bytes 2621440 | tf_op jit(solution)/shard_map/reshape | solution.py:520
  9.7 104.7 %shard_map.118 = (bf16[320,1024]{1,0:T(8,128)(2,1)}, bf16[320,1024]{1,0:T(8,128)(2,1)}, f32[8,384]{1,0:T(8,128)}, f32[80,2880]{1,0:T(8,128)}, f32[80,2880]{1,0:T(8,128)}) custom-call(bf16[320,1024]{1,0:T(8,128)(2,1)} %get-tuple-element.41.x, bf16[320,1024]{1,0:T(8,128)(2,1)} %get-tuple-element.40.g, f32[320,8]{1,0:T(8,128)} %copy.32.pv, ...), custom_call_target="tpu_custom_call" | custom-call | tf_op jit(solution)/shard_map/pallas_call | solution.py:483
  114.4 0.0 copy-start.5
  114.4 0.0 copy-start.1
  114.4 2.1 %copy.41 = bf16[40,8,8,128]{3,2,1,0:T(8,128)(2,1)} copy(bf16[40,8,8,128]{3,1,2,0:T(8,128)(2,1)} %bitcast.36) | data formatting | bytes 1310720
  116.5 2.0 %copy.42 = bf16[40,8,8,128]{3,2,1,0:T(8,128)(2,1)} copy(bf16[40,8,8,128]{3,1,2,0:T(8,128)(2,1)} %bitcast.35) | data formatting | bytes 1310720
  118.6 0.0 copy-done.5
  118.6 0.6 slice.22
  119.1 0.6 slice.23
  119.7 0.0 copy-done.1
  119.7 0.4 copy.35
  120.2 0.0 copy-start
  120.2 1.5 %copy.37 = f32[80,9,320]{2,0,1:T(8,128)} copy(f32[80,9,320]{0,2,1:T(8,128)S(1)} %bitcast.27) | data formatting | bytes 1843200
  121.7 0.0 copy-done
  121.7 0.4 copy.36
  122.2 1.5 %copy.38 = f32[80,9,320]{2,0,1:T(8,128)} copy(f32[80,9,320]{0,2,1:T(8,128)S(1)} %bitcast.28) | data formatting | bytes 1843200
  (3 shorter events, 0.0 us)
Async XLA Ops:
  0.6 6.3 %copy-start.4 = (bf16[80,9,320]{2,0,1:T(8,128)(2,1)S(1)}, bf16[80,9,320]{2,0,1:T(8,128)(2,1)}, u32[]{:S(2)}) copy-start(bf16[80,9,320]{2,0,1:T(8,128)(2,1)} %param.10) | copy-start | bytes 1382404
  6.9 1.5 %copy-start.2 = (bf16[1,320,8,128]{3,2,1,0:T(8,128)(2,1)S(1)}, bf16[1,320,8,128]{3,2,1,0:T(8,128)(2,1)}, u32[]{:S(2)}) copy-start(bf16[1,320,8,128]{3,2,1,0:T(8,128)(2,1)} %param.13) | copy-start | bytes 1966084
  6.9 1.5 %copy-start.3 = (bf16[1,320,8,128]{3,2,1,0:T(8,128)(2,1)S(1)}, bf16[1,320,8,128]{3,2,1,0:T(8,128)(2,1)}, u32[]{:S(2)}) copy-start(bf16[1,320,8,128]{3,2,1,0:T(8,128)(2,1)} %param.7) | copy-start | bytes 1966084
  114.4 4.2 %copy-start.5 = (f32[8,384]{1,0:T(8,128)S(1)}, f32[8,384]{1,0:T(8,128)}, u32[]{:S(2)}) copy-start(f32[8,384]{1,0:T(8,128)} %get-tuple-element.13) | copy-start | bytes 36868
  114.4 5.4 %copy-start.1 = (f32[80,2880]{1,0:T(8,128)S(1)}, f32[80,2880]{1,0:T(8,128)}, u32[]{:S(2)}) copy-start(f32[80,2880]{1,0:T(8,128)} %get-tuple-element.14) | copy-start | bytes 2764804
  120.2 1.5 %copy-start = (f32[80,2880]{1,0:T(8,128)S(1)}, f32[80,2880]{1,0:T(8,128)}, u32[]{:S(2)}) copy-start(f32[80,2880]{1,0:T(8,128)} %get-tuple-element.15) | copy-start | bytes 2764804

commit v2 on v1

--- a/solution.py
+++ b/solution.py
@@ -1,7 +1,6 @@
-import functools
-
 import jax
 import jax.numpy as jnp
+import numpy as np
 from jax import lax
 from jax.experimental import pallas as pl
 from jax.experimental.pallas import tpu as pltpu
@@ -16,16 +15,17 @@
 
 
 def block_kernel(
-    x, g, pv, w1s, w2s, pool, spread,
+    x, g, gains, biases, shift, w1s, w2s, pool, spread,
     out, gin, small, dw1, dw2,
-    act_stack, mid_stack, cot_stack, wfull1, wfull2, wturn,
+    act_stack, mid_stack, cot_stack, wfull1, wfull2, wturn1, wturn2,
     normed1, normed2, back, hgrad, cols, stat, halo_out, halo_in,
-    part, core_in, core_keep, x_in, z_out, z_in, z_all, tiny, tiny_x,
+    part, core_in, core_keep, x_in, z_out, z_in, z_all, flat, vectors, tiny, tiny_x,
     send, recv,
 ):
     channels, cells = x.shape
     height = cells // LANES
-    shard = w1s.shape[0]
+    taps, shard, _ = w1s.shape
+    depth = taps * channels
     rows = lax.axis_size("rows")
     row = lax.axis_index("rows")
     zero = lax.axis_index("zero")
@@ -161,9 +161,15 @@
     for target in (mate, over):
         pl.semaphore_signal(barrier, inc=1, device_id={"zero": target}, device_id_type=MESH)
 
+    vectors[...] = jnp.zeros_like(vectors)
+    vectors[0:2, 0:channels] = gains[...]
+    vectors[2:4, 0:channels] = biases[...]
+    vectors[4:5, 0:channels] = shift[...]
+    pv = vectors[...].T[:channels, :]
+    GAIN1, GAIN2 = pv[:, 0:1], pv[:, 1:2]
     SUM_A, SUM_B, SUM_C, SUM_D, SUM_T = 13, 14, 15, 16, 17
     for i in range(5):
-        column(8 + i, pv[:, i : i + 1])
+        column((8, 10, 9, 11, 12)[i], pv[:, i : i + 1])
 
     def first_sums(start):
         total = jnp.zeros((shard, LANES), F32)
@@ -181,19 +187,20 @@
     stat0 = stat_start(0, s0, s1)
     halo_g = halo_start(0, g.at[:, 0:LANES], g.at[:, (height - 1) * LANES : height * LANES])
 
-    def gather_start(own, full):
-        near = go(own, full.at[zero], {"zero": mate})
-        far = go(own, full.at[zero], {"zero": over})
-        return near, far
+    def flatten(own, full):
+        full[zero] = jnp.concatenate([own[tap] for tap in range(taps)], axis=1)
+
+    def gather_start(full, target):
+        return go(full.at[zero], full.at[zero], {"zero": target})
 
     def gather_pass(full, far):
         far.wait_recv()
         return go(full.at[over], full.at[over], {"zero": mate})
 
-    gather1 = gather_start(w1s, wfull1)
-    gather2 = gather_start(w2s, wfull2)
-    wfull1[zero] = w1s[...]
-    wfull2[zero] = w2s[...]
+    flatten(w1s, wfull1)
+    far1 = gather_start(wfull1, over)
+    near1 = gather_start(wfull1, mate)
+    flatten(w2s, wfull2)
 
     moments(0, stat0, 0)
 
@@ -217,9 +224,11 @@
             put(cot_stack, g[pl.ds(start, shard), line(h)].astype(F32), start, h + 1, True)
     chunked(cot_fill)
     halo_finish(0, halo_g, cot_stack, True)
-    pass1 = gather_pass(wfull1, gather1[1])
+    pass1 = gather_pass(wfull1, far1)
+    far2 = gather_start(wfull2, over)
+    near2 = gather_start(wfull2, mate)
     halo_finish(1, halo_a, act_stack, False)
-    gather1[0].wait_recv()
+    near1.wait_recv()
     pass1.wait_recv()
 
     TILE = 256
@@ -255,14 +264,13 @@
 
     PAIR = 2 * channels
 
-    def turn(full):
-        depth = full.shape[2]
+    def turn(full, wturn):
         for begin in range(0, depth, PAIR):
             end = min(begin + PAIR, depth)
             weights = full[:, :, begin:end].reshape(channels, end - begin)
             wturn[begin:end, :] = weights.T
 
-    def conv_back(stack):
+    def conv_back(stack, wturn):
         def tile(at):
             total = jnp.zeros((channels, TILE), F32)
             for tap in range(9):
@@ -271,11 +279,12 @@
             back[:, at] = total
         tiles(tile)
 
-    pass2 = gather_pass(wfull2, gather2[1])
-    gather2[0].wait_recv()
+    pass2 = gather_pass(wfull2, far2)
+    turn(wfull1, wturn1)
+    near2.wait_recv()
     pass2.wait_recv()
-    turn(wfull2)
-    conv_back(cot_stack)
+    turn(wfull2, wturn2)
+    conv_back(cot_stack, wturn2)
     moments(1, stat1, 2)
 
     def second_act(start):
@@ -300,67 +309,107 @@
     chunked(second_act)
     halo_b = halo_start(2, halo_out.at[1, 0], halo_out.at[1, 1])
     gain_cross2, bias_sum2 = lane_sum(cols[SUM_C]), lane_sum(cols[SUM_D])
-    stat2 = stat_start(2, pv[:, 2:3] * bias_sum2, pv[:, 2:3] * gain_cross2)
+    stat2 = stat_start(2, GAIN2 * bias_sum2, GAIN2 * gain_cross2)
     halo_finish(2, halo_b, mid_stack, False)
 
-    depth = w1s.shape[1]
-
-    def weight_grad(which, cot, stack):
-        for begin in range(0, depth, PAIR):
-            end = min(begin + PAIR, depth)
+    span = part.shape[3]
+    piece = z_out.shape[3]
+    steps = [1 << k for k in range(rows.bit_length() - 1)]
+
+    def extent(stream):
+        begin = stream % 2 * span
+        return begin, min(begin + span, depth)
+
+    def weight_grad(stream, cot, stack):
+        first, last = extent(stream)
+        half = span // 2
+        for begin in range(first, last, half):
+            end = min(begin + half, last)
             value = lax.dot_general(
                 cot[...], stack[begin:end, :], (((1,), (1,)), ((), ())), preferred_element_type=F32
             )
-            part[which, :, :, begin:end] = value.astype(BF16).reshape(blocks, shard, end - begin)
+            part[stream, :, :, begin - first : end - first] = value.astype(BF16).reshape(
+                blocks, shard, end - begin
+            )
         return [
-            go(part.at[which, mate], core_in.at[which, 0], {"zero": mate}),
-            go(part.at[which, over_mate], core_in.at[which, 1], {"zero": mate}),
+            go(part.at[stream, over_mate], core_in.at[stream, 1], {"zero": mate}),
+            go(part.at[stream, mate], core_in.at[stream, 0], {"zero": mate}),
         ]
 
-    def reduce_core(which, copies):
+    def reduce_core(stream, copies):
+        copies[0].wait_recv()
+        core_keep[stream] = (
+            part[stream, over].astype(F32) + core_in[stream, 1].astype(F32)
+        ).astype(BF16)
+        return copies[1], go(core_keep.at[stream], x_in.at[stream], {"zero": over})
+
+    def rows_send(stream, k, start, count):
+        bit = lax.rem(lax.div(row, steps[k]), 2)
+        half = count // 2
+        keep = start + bit * half
+        give = start + (1 - bit) * half
+        offset = rows - count
+        copy = go(
+            z_out.at[stream, pl.ds(give, half)],
+            z_in.at[stream, pl.ds(offset, half)],
+            {"rows": row + steps[k] * (1 - 2 * bit)},
+        )
+        return copy, k, keep, half, offset
+
+    def reduce_over(stream, copies):
         for copy in copies:
             copy.wait_recv()
-        core_keep[which] = (
-            part[which, over].astype(F32) + core_in[which, 1].astype(F32)
+        value = (
+            part[stream, zero].astype(F32)
+            + core_in[stream, 0].astype(F32)
+            + x_in[stream].astype(F32)
         ).astype(BF16)
-        return go(core_keep.at[which], x_in.at[which], {"zero": over})
-
-    piece = z_out.shape[3]
-
-    def reduce_over(which, copy):
+        for q in range(-(-span // piece)):
+            z_out[stream, q] = value[:, q * piece : (q + 1) * piece]
+        return rows_send(stream, 0, 0, rows)
+
+    def reduce_step(stream, state):
+        copy, k, keep, half, offset = state
         copy.wait_recv()
-        value = (
-            part[which, zero].astype(F32)
-            + core_in[which, 0].astype(F32)
-            + x_in[which].astype(F32)
-        ).astype(BF16)
-        for q in range(-(-depth // piece)):
-            end = min((q + 1) * piece, depth)
-            z_out[which, q, :, : end - q * piece] = value[:, q * piece : end]
-        copies = []
-        for d in range(1, rows):
-            to = lax.rem(row + d, rows)
-            copies.append(go(z_out.at[which, to], z_in.at[which, row], {"rows": to}))
-        return copies
-
-    def reduce_rows(which, copies):
-        for copy in copies:
-            copy.wait_recv()
-        z_in[which, row] = z_out[which, row]
-        total = z_in[which, 0].astype(F32)
-        for i in range(1, rows):
-            total = total + z_in[which, i].astype(F32)
-        z_all[which, row] = total.astype(BF16)
-        return to_rows(z_all.at[which, row], z_all.at[which, row])
-
-    def reduce_finish(which, copies, target):
-        for copy in copies:
-            copy.wait_recv()
-        for q in range(-(-depth // piece)):
-            end = min((q + 1) * piece, depth)
-            target[:, q * piece : end] = z_all[which, q, :, : end - q * piece].astype(F32)
-
-    grad2 = weight_grad(1, g, mid_stack)
+        last = k + 1 == len(steps)
+        for i in range(half):
+            value = (
+                z_out[stream, keep + i].astype(F32) + z_in[stream, offset + i].astype(F32)
+            ).astype(BF16)
+            if last:
+                z_all[stream, keep + i] = value
+            else:
+                z_out[stream, keep + i] = value
+        if last:
+            return gather_step(stream, k, keep, half)
+        return rows_send(stream, k + 1, keep, half)
+
+    def gather_step(stream, k, start, count):
+        bit = lax.rem(lax.div(row, steps[k]), 2)
+        at = pl.ds(start, count)
+        copy = go(
+            z_all.at[stream, at], z_all.at[stream, at], {"rows": row + steps[k] * (1 - 2 * bit)}
+        )
+        return copy, k, start - bit * count, 2 * count
+
+    def spread_step(stream, state):
+        copy, k, start, count = state
+        copy.wait_recv()
+        if k == 0:
+            return None
+        return gather_step(stream, k - 1, start, count)
+
+    def reduce_finish(which, target):
+        for stream in (2 * which, 2 * which + 1):
+            first, last = extent(stream)
+            for q in range(-(-(last - first) // piece)):
+                begin = first + q * piece
+                flat[which, :, begin : begin + piece] = z_all[stream, q].astype(F32)
+        for tap in range(taps):
+            target[tap] = flat[which, :, tap * channels : (tap + 1) * channels]
+
+    s2 = weight_grad(2, g, mid_stack)
+    s3 = weight_grad(3, g, mid_stack)
 
     average, cross = stat_finish(2, stat2)
     column(4, average)
@@ -388,13 +437,24 @@
     halo_h = halo_start(3, halo_out.at[2, 0], halo_out.at[2, 1])
     time_sum = lane_sum(cols[SUM_T])
 
-    grad2 = reduce_core(1, grad2)
-    grad1 = weight_grad(0, hgrad, act_stack)
-    turn(wfull1)
+    s2 = reduce_core(2, s2)
+    s3 = reduce_core(3, s3)
+    s0 = weight_grad(0, hgrad, act_stack)
+    s2 = reduce_over(2, s2)
+    s1 = weight_grad(1, hgrad, act_stack)
+    s0 = reduce_core(0, s0)
+    s3 = reduce_over(3, s3)
     halo_finish(3, halo_h, cot_stack, True)
-    conv_back(cot_stack)
-    grad1 = reduce_core(0, grad1)
-    grad2 = reduce_over(1, grad2)
+    s1 = reduce_core(1, s1)
+    s2 = reduce_step(2, s2)
+    conv_back(cot_stack, wturn1)
+    s0 = reduce_over(0, s0)
+    s3 = reduce_step(3, s3)
+    for _ in steps[1:]:
+        s2 = reduce_step(2, s2)
+    s1 = reduce_over(1, s1)
+    for _ in steps[1:]:
+        s3 = reduce_step(3, s3)
 
     def first_slope(start):
         at = pl.ds(start, shard)
@@ -410,7 +470,7 @@
         cols[SUM_B, at, :] = sums[1]
     chunked(first_slope)
     gain_cross1, bias_sum1 = lane_sum(cols[SUM_A]), lane_sum(cols[SUM_B])
-    stat3 = stat_start(3, pv[:, 0:1] * bias_sum1, pv[:, 0:1] * gain_cross1)
+    stat3 = stat_start(3, GAIN1 * bias_sum1, GAIN1 * gain_cross1)
     packed = jnp.zeros((channels, LANES), F32)
     for i, value in enumerate((time_sum, gain_cross1, bias_sum1, gain_cross2, bias_sum2)):
         packed = jnp.where(wide == i, value, packed)
@@ -422,7 +482,8 @@
         out[:, at] = (x[:, at].astype(F32) + value).astype(BF16)
     conv(wfull2, mid_stack, emit_out)
 
-    grad1 = reduce_over(0, grad1)
+    s0 = reduce_step(0, s0)
+    s1 = reduce_step(1, s1)
     average, cross = stat_finish(3, stat3)
     column(6, average)
     column(7, cross)
@@ -434,7 +495,11 @@
         total = total + tiny[i]
     tiny_x[0] = total
     first_hop = go(tiny_x.at[0], tiny_x.at[1], {"zero": mate})
-    grad2 = reduce_rows(1, grad2)
+    for _ in steps[1:]:
+        s0 = reduce_step(0, s0)
+        s1 = reduce_step(1, s1)
+    s2 = spread_step(2, s2)
+    s3 = spread_step(3, s3)
 
     def input_back(start):
         at = pl.ds(start, shard)
@@ -450,12 +515,19 @@
     first_hop.wait_recv()
     tiny_x[2] = total + tiny_x[1]
     second_hop = go(tiny_x.at[2], tiny_x.at[3], {"zero": over})
-    grad1 = reduce_rows(0, grad1)
+    for _ in steps[1:]:
+        s2 = spread_step(2, s2)
+        s3 = spread_step(3, s3)
+    s0 = spread_step(0, s0)
+    s1 = spread_step(1, s1)
+    reduce_finish(1, dw2)
     second_hop.wait_recv()
     pick = lax.broadcasted_iota(jnp.int32, total.shape, 0)
     small[...] = jnp.where(pick == 0, total, tiny_x[2] + tiny_x[3])
-    reduce_finish(1, grad2, dw2)
-    reduce_finish(0, grad1, dw1)
+    for _ in steps[1:]:
+        s0 = spread_step(0, s0)
+        s1 = spread_step(1, s1)
+    reduce_finish(0, dw1)
     for copy in pending:
         copy.wait_send()
 
@@ -467,23 +539,20 @@
     depth = taps * channels
     rows = lax.axis_size("rows")
     blocks = channels // shard
-    vectors = jnp.stack(
-        [norm_gains[0], norm_biases[0], norm_gains[1], norm_biases[1], time_shift[0]]
-        + [jnp.zeros((channels,), F32)] * 3,
-        axis=1,
-    )
-    group = jnp.arange(channels) // (channels // NORM_GROUPS)
-    pool = (group[None, :] == jnp.arange(NORM_GROUPS)[:, None]).astype(F32)
-    piece = -(-depth // (rows * LANES)) * LANES
+    group = np.arange(channels) // (channels // NORM_GROUPS)
+    pool = (group[None, :] == np.arange(NORM_GROUPS)[:, None]).astype(np.float32)
+    levels = rows.bit_length() - 1
+    span = -(-depth // (8 * LANES)) * 4 * LANES
+    piece = -(-span // (rows * LANES)) * LANES
     padded = -(-channels // LANES) * LANES
     vmem = pl.BlockSpec(memory_space=pltpu.VMEM)
-    copies = 4 * (rows - 1) + 8 + 6 + 6 + 5 * (rows - 1) + 8
+    copies = 5 * (rows - 1) + 8 + 6 + 4 * (3 + 2 * levels) + 2
     field = jax.ShapeDtypeStruct((channels, cells), BF16)
-    grads = jax.ShapeDtypeStruct((shard, depth), F32)
+    grads = jax.ShapeDtypeStruct((taps, shard, channels), F32)
     out, gin, small, dw1, dw2 = pl.pallas_call(
         block_kernel,
         out_shape=(field, field, jax.ShapeDtypeStruct((8, padded), F32), grads, grads),
-        in_specs=[vmem] * 7,
+        in_specs=[vmem] * 9,
         out_specs=(vmem,) * 5,
         scratch_shapes=[
             pltpu.VMEM((depth, cells), BF16),
@@ -491,6 +560,7 @@
             pltpu.VMEM((depth, cells), BF16),
             pltpu.VMEM((blocks, shard, depth), BF16),
             pltpu.VMEM((blocks, shard, depth), BF16),
+            pltpu.VMEM((depth, channels), BF16),
             pltpu.VMEM((depth, channels), BF16),
             pltpu.VMEM((channels, cells), F32),
             pltpu.VMEM((channels, cells), F32),
@@ -500,13 +570,15 @@
             pltpu.VMEM((4, rows, NORM_GROUPS, LANES), F32),
             pltpu.VMEM((3, 2, channels, LANES), BF16),
             pltpu.VMEM((4, 2, channels, LANES), BF16),
-            pltpu.VMEM((2, blocks, shard, depth), BF16),
-            pltpu.VMEM((2, 2, shard, depth), BF16),
-            pltpu.VMEM((2, shard, depth), BF16),
-            pltpu.VMEM((2, shard, depth), BF16),
-            pltpu.VMEM((2, rows, shard, piece), BF16),
-            pltpu.VMEM((2, rows, shard, piece), BF16),
-            pltpu.VMEM((2, rows, shard, piece), BF16),
+            pltpu.VMEM((4, blocks, shard, span), BF16),
+            pltpu.VMEM((4, 2, shard, span), BF16),
+            pltpu.VMEM((4, shard, span), BF16),
+            pltpu.VMEM((4, shard, span), BF16),
+            pltpu.VMEM((4, rows, shard, piece), BF16),
+            pltpu.VMEM((4, rows, shard, piece), BF16),
+            pltpu.VMEM((4, rows, shard, piece), BF16),
+            pltpu.VMEM((2, shard, 2 * span), F32),
+            pltpu.VMEM((LANES, padded), F32),
             pltpu.VMEM((rows, 8, padded), F32),
             pltpu.VMEM((4, 8, padded), F32),
             pltpu.SemaphoreType.DMA((copies,)),
@@ -518,18 +590,20 @@
     )(
         latents.reshape(channels, cells),
         grad_output.reshape(channels, cells),
-        vectors,
-        conv_first.reshape(shard, depth),
-        conv_second.reshape(shard, depth),
-        pool,
-        pool.T,
+        norm_gains,
+        norm_biases,
+        time_shift,
+        jnp.transpose(conv_first, (1, 0, 2)),
+        jnp.transpose(conv_second, (1, 0, 2)),
+        jnp.asarray(pool),
+        jnp.asarray(np.ascontiguousarray(pool.T)),
     )
     return (
         out.reshape(latents.shape),
         gin.reshape(latents.shape),
         small[0:1, :channels],
-        dw1.reshape(conv_first.shape),
-        dw2.reshape(conv_second.shape),
+        jnp.transpose(dw1, (1, 0, 2)),
+        jnp.transpose(dw2, (1, 0, 2)),
         small[1:5, :channels],
     )
 

time: 124 us -> 112 us (0.903)
  local copies, waits for them, and re-layouts: 16.9 us -> 9.59 us
  Pallas kernels: 105 us -> 102 us
  other arithmetic: 1.41 us -> 0 us
    unnamed x18 -> x12, local copies, waits for them, and re-layouts: 9.08 us -> 5.78 us
    pallas_call x1, Pallas kernels: 105 us -> 102 us  [local(): pl.pallas_call(block_kernel, out_shape=(field, field, jax.ShapeDtypeStruc...]
    another operation x5 -> x0, local copies, waits for them, and re-layouts: 2.32 us -> none  [local(): jnp.stack([norm_gains[0], norm_biases[0], norm_gains[1], norm_biases[1],...]
    reshape x2 -> x0, local copies, waits for them, and re-layouts: 2.1 us -> none  [the longest x1 1.05 us: local(): conv_second.reshape(shard, depth)]
    convert_element_type x2 -> x0, other arithmetic: 1.4 us -> none  [local(): pool = (group[None, :] == jnp.arange(NORM_GROUPS)[:, None]).astype(F32)]
    reshape x1, local copies, waits for them, and re-layouts: 1.37 us -> 2.65 us  [local(): grad_output.reshape(channels, cells)]
where the time goes in v2:
time: 112 us
  Pallas kernels  102 us (91%)
  local copies, waits for them, and re-layouts  9.59 us (9%)
    pallas_call x1, Pallas kernels, local(): pl.pallas_call(block_kernel, out_shape=(field, field, jax.ShapeDtypeStruc...  102 us
    unnamed x12, local copies, waits for them, and re-layouts  5.78 us
    reshape x1, local copies, waits for them, and re-layouts, local(): grad_output.reshape(channels, cells)  2.65 us

profile of v2, /device:TPU:0, one launch (start us, length us, event | category | flops | bytes accessed | tf_op | source)
XLA Modules:
  0.0 112.1 jit_solution(1676450563773582722)
XLA Ops:
  0.6 2.7 %copy_bitcast_fusion = (bf16[320,1024]{1,0:T(8,128)(2,1)}, bf16[320,1024]{1,0:T(8,128)(2,1)}) fusion(bf16[40,8,8,128]{3,2,1,0:T(8,128)(2,1)} %bitcast.20, bf16[40,8,8,128]{3,2,1,0:T(8,128)(2,1)} %bitcast.21), kind=kLoop, calls=%fused_computation | loop fusion | bytes 2621440 | tf_op jit(solution)/shard_map/reshape | solution.py:592
  3.3 101.8 %shard_map.136 = (bf16[320,1024]{1,0:T(8,128)(2,1)}, bf16[320,1024]{1,0:T(8,128)(2,1)}, f32[8,384]{1,0:T(8,128)}, f32[9,80,320]{2,1,0:T(8,128)}, f32[9,80,320]{2,1,0:T(8,128)}) custom-call(bf16[320,1024]{1,0:T(8,128)(2,1)} %get-tuple-element.17.x, bf16[320,1024]{1,0:T(8,128)(2,1)} %get-tuple-element.16.g, f32[2,320]{1,0:T(2,128)} %gains.1, f32[2,320]{1,0:T(2,128)} %biases.1, ...), custom_call_target="tpu_custom_call" | custom-call | tf_op jit(solution)/shard_map/pallas_call | solution.py:552
  105.1 0.0 copy-start.2
  105.1 0.0 copy-start.3
  105.1 0.0 copy-start.1
  105.1 2.2 %copy.17 = bf16[40,8,8,128]{3,2,1,0:T(8,128)(2,1)} copy(bf16[40,8,8,128]{3,1,2,0:T(8,128)(2,1)} %bitcast.25) | data formatting | bytes 1310720
  107.3 0.0 copy-done.2
  107.3 1.0 copy.18
  108.3 0.0 copy-done.3
  108.3 0.6 slice.6
  108.8 0.6 slice.7
  109.4 0.0 copy-done.1
  109.4 0.0 copy-start
  109.4 1.0 copy.23
  110.4 0.7 copy-done
  111.1 1.0 copy.24
Async XLA Ops:
  105.1 2.2 %copy-start.2 = (bf16[320,1024]{1,0:T(8,128)(2,1)S(1)}, bf16[320,1024]{1,0:T(8,128)(2,1)}, u32[]{:S(2)}) copy-start(bf16[320,1024]{1,0:T(8,128)(2,1)} %get-tuple-element.12) | copy-start | bytes 1966084
  105.1 3.2 %copy-start.3 = (f32[8,384]{1,0:T(8,128)S(1)}, f32[8,384]{1,0:T(8,128)}, u32[]{:S(2)}) copy-start(f32[8,384]{1,0:T(8,128)} %get-tuple-element.13) | copy-start | bytes 36868
  105.1 4.3 %copy-start.1 = (f32[9,80,320]{2,1,0:T(8,128)S(1)}, f32[9,80,320]{2,1,0:T(8,128)}, u32[]{:S(2)}) copy-start(f32[9,80,320]{2,1,0:T(8,128)} %get-tuple-element.14) | copy-start | bytes 2764804
  109.4 1.6 %copy-start = (f32[9,80,320]{2,1,0:T(8,128)S(1)}, f32[9,80,320]{2,1,0:T(8,128)}, u32[]{:S(2)}) copy-start(f32[9,80,320]{2,1,0:T(8,128)} %get-tuple-element.15) | copy-start | bytes 2764804

commit v3 on v2

--- a/solution.py
+++ b/solution.py
@@ -233,17 +233,19 @@
 
     TILE = 256
 
-    def tiles(body):
+    count = cells // TILE
+
+    def tiles(body, first=0, last=count):
         def step(i, _):
             body(pl.ds(pl.multiple_of(i * TILE, TILE), TILE))
             return 0
-        lax.fori_loop(0, cells // TILE, step, 0)
-
-    def conv(full, stack, emit):
+        lax.fori_loop(first, last, step, 0)
+
+    def conv(full, stack, emit, first=0, last=count):
         def tile(at):
             weights = full[...].reshape(channels, full.shape[2])
             emit(at, jnp.dot(weights, stack[:, at], preferred_element_type=F32))
-        tiles(tile)
+        tiles(tile, first, last)
 
     def emit_hidden(at, value):
         shift = cols[12][:, 0:1]
@@ -268,14 +270,14 @@
         for begin in range(0, depth, PAIR):
             end = min(begin + PAIR, depth)
             weights = full[:, :, begin:end].reshape(channels, end - begin)
-            wturn[begin:end, :] = weights.T
+            turned = weights.T
+            wturn[:, begin:end] = jnp.concatenate(
+                [turned[i : i + channels] for i in range(0, end - begin, channels)], axis=1
+            )
 
     def conv_back(stack, wturn):
         def tile(at):
-            total = jnp.zeros((channels, TILE), F32)
-            for tap in range(9):
-                span = slice(tap * channels, (tap + 1) * channels)
-                total = total + jnp.dot(wturn[span, :], stack[span, at], preferred_element_type=F32)
+            total = jnp.dot(wturn[...], stack[:, at], preferred_element_type=F32)
             back[:, at] = total
         tiles(tile)
 
@@ -452,9 +454,6 @@
     s3 = reduce_step(3, s3)
     for _ in steps[1:]:
         s2 = reduce_step(2, s2)
-    s1 = reduce_over(1, s1)
-    for _ in steps[1:]:
-        s3 = reduce_step(3, s3)
 
     def first_slope(start):
         at = pl.ds(start, shard)
@@ -471,6 +470,10 @@
     chunked(first_slope)
     gain_cross1, bias_sum1 = lane_sum(cols[SUM_A]), lane_sum(cols[SUM_B])
     stat3 = stat_start(3, GAIN1 * bias_sum1, GAIN1 * gain_cross1)
+    s1 = reduce_over(1, s1)
+    s0 = reduce_step(0, s0)
+    for _ in steps[1:]:
+        s3 = reduce_step(3, s3)
     packed = jnp.zeros((channels, LANES), F32)
     for i, value in enumerate((time_sum, gain_cross1, bias_sum1, gain_cross2, bias_sum2)):
         packed = jnp.where(wide == i, value, packed)
@@ -480,10 +483,17 @@
 
     def emit_out(at, value):
         out[:, at] = (x[:, at].astype(F32) + value).astype(BF16)
-    conv(wfull2, mid_stack, emit_out)
-
-    s0 = reduce_step(0, s0)
+    conv(wfull2, mid_stack, emit_out, 0, count // 2)
     s1 = reduce_step(1, s1)
+    for _ in steps[1:]:
+        s0 = reduce_step(0, s0)
+    s2 = spread_step(2, s2)
+    conv(wfull2, mid_stack, emit_out, count // 2, count)
+    for _ in steps[1:]:
+        s1 = reduce_step(1, s1)
+    s3 = spread_step(3, s3)
+    s0 = spread_step(0, s0)
+
     average, cross = stat_finish(3, stat3)
     column(6, average)
     column(7, cross)
@@ -495,12 +505,6 @@
         total = total + tiny[i]
     tiny_x[0] = total
     first_hop = go(tiny_x.at[0], tiny_x.at[1], {"zero": mate})
-    for _ in steps[1:]:
-        s0 = reduce_step(0, s0)
-        s1 = reduce_step(1, s1)
-    s2 = spread_step(2, s2)
-    s3 = spread_step(3, s3)
-
     def input_back(start):
         at = pl.ds(start, shard)
         for h in range(height):
@@ -518,7 +522,6 @@
     for _ in steps[1:]:
         s2 = spread_step(2, s2)
         s3 = spread_step(3, s3)
-    s0 = spread_step(0, s0)
     s1 = spread_step(1, s1)
     reduce_finish(1, dw2)
     second_hop.wait_recv()
@@ -560,8 +563,8 @@
             pltpu.VMEM((depth, cells), BF16),
             pltpu.VMEM((blocks, shard, depth), BF16),
             pltpu.VMEM((blocks, shard, depth), BF16),
-            pltpu.VMEM((depth, channels), BF16),
-            pltpu.VMEM((depth, channels), BF16),
+            pltpu.VMEM((channels, depth), BF16),
+            pltpu.VMEM((channels, depth), BF16),
             pltpu.VMEM((channels, cells), F32),
             pltpu.VMEM((channels, cells), F32),
             pltpu.VMEM((channels, cells), F32),

time: 112 us -> 109 us (0.973)
  Pallas kernels: 102 us -> 98.1 us
    pallas_call x1, Pallas kernels: 102 us -> 98.1 us  [local(): pl.pallas_call(block_kernel, out_shape=(field, field, jax.ShapeDtypeStruc...]
where the time goes in v3:
time: 109 us; the launch traced here: 108 us
  Pallas kernels  98.1 us (90%)
  local copies, waits for them, and re-layouts  9.59 us (9%)
    pallas_call x1, Pallas kernels, local(): pl.pallas_call(block_kernel, out_shape=(field, field, jax.ShapeDtypeStruc...  98.1 us
    unnamed x12, local copies, waits for them, and re-layouts  5.78 us
    reshape x1, local copies, waits for them, and re-layouts, local(): grad_output.reshape(channels, cells)  2.65 us

profile of v3, /device:TPU:0, one launch (start us, length us, event | category | flops | bytes accessed | tf_op | source)
XLA Modules:
  0.0 108.4 jit_solution(6786001480974402169)
XLA Ops:
  0.6 2.7 %copy_bitcast_fusion = (bf16[320,1024]{1,0:T(8,128)(2,1)}, bf16[320,1024]{1,0:T(8,128)(2,1)}) fusion(bf16[40,8,8,128]{3,2,1,0:T(8,128)(2,1)} %bitcast.20, bf16[40,8,8,128]{3,2,1,0:T(8,128)(2,1)} %bitcast.21), kind=kLoop, calls=%fused_computation | loop fusion | bytes 2621440 | tf_op jit(solution)/shard_map/reshape | solution.py:595
  3.3 98.1 %shard_map.136 = (bf16[320,1024]{1,0:T(8,128)(2,1)}, bf16[320,1024]{1,0:T(8,128)(2,1)}, f32[8,384]{1,0:T(8,128)}, f32[9,80,320]{2,1,0:T(8,128)}, f32[9,80,320]{2,1,0:T(8,128)}) custom-call(bf16[320,1024]{1,0:T(8,128)(2,1)} %get-tuple-element.17.x, bf16[320,1024]{1,0:T(8,128)(2,1)} %get-tuple-element.16.g, f32[2,320]{1,0:T(2,128)} %gains.1, f32[2,320]{1,0:T(2,128)} %biases.1, ...), custom_call_target="tpu_custom_call" | custom-call | tf_op jit(solution)/shard_map/pallas_call | solution.py:555
  101.4 0.0 copy-start.2
  101.4 0.0 copy-start.3
  101.4 0.0 copy-start.1
  101.4 2.2 %copy.17 = bf16[40,8,8,128]{3,2,1,0:T(8,128)(2,1)} copy(bf16[40,8,8,128]{3,1,2,0:T(8,128)(2,1)} %bitcast.25) | data formatting | bytes 1310720
  103.6 0.0 copy-done.2
  103.6 1.0 copy.18
  104.6 0.0 copy-done.3
  104.6 0.6 slice.6
  105.1 0.6 slice.7
  105.7 0.0 copy-done.1
  105.7 0.0 copy-start
  105.7 1.0 copy.23
  106.7 0.7 copy-done
  107.4 1.0 copy.24
Async XLA Ops:
  101.4 2.2 %copy-start.2 = (bf16[320,1024]{1,0:T(8,128)(2,1)S(1)}, bf16[320,1024]{1,0:T(8,128)(2,1)}, u32[]{:S(2)}) copy-start(bf16[320,1024]{1,0:T(8,128)(2,1)} %get-tuple-element.12) | copy-start | bytes 1966084
  101.4 3.2 %copy-start.3 = (f32[8,384]{1,0:T(8,128)S(1)}, f32[8,384]{1,0:T(8,128)}, u32[]{:S(2)}) copy-start(f32[8,384]{1,0:T(8,128)} %get-tuple-element.13) | copy-start | bytes 36868
  101.4 4.3 %copy-start.1 = (f32[9,80,320]{2,1,0:T(8,128)S(1)}, f32[9,80,320]{2,1,0:T(8,128)}, u32[]{:S(2)}) copy-start(f32[9,80,320]{2,1,0:T(8,128)} %get-tuple-element.14) | copy-start | bytes 2764804
  105.7 1.6 %copy-start = (f32[9,80,320]{2,1,0:T(8,128)S(1)}, f32[9,80,320]{2,1,0:T(8,128)}, u32[]{:S(2)}) copy-start(f32[9,80,320]{2,1,0:T(8,128)} %get-tuple-element.15) | copy-start | bytes 2764804
